TPU v7x, 256 devices: a whole 4x4x8 slice. The times are simulated.
256 devices in a mesh: seq: 32 (over z, y), head: 8 (over x, core).
Axes of the slice: x: 4, y: 4, z: 8, core: 2. Of those that a mesh axis runs over, the one named last changes fastest.
Arguments:
- queries: bfloat16 [16384, 32, 128], P('seq', 'head'), may hold values from -6 to 6
- key_matrix: bfloat16 [16384, 32, 128], P('seq', 'head'), may hold values from -6 to 6
- value_matrix: bfloat16 [16384, 32, 128], P('seq', 'head'), may hold values from -6 to 6
- level_weight: float32 [15, 32, 16384], P(None, 'head', 'seq'), may hold values from 0.25 to 4
- out_weight: bfloat16 [32, 128, 4096], P('head'), may hold values from -0.09375 to 0.09375
- grad_out: bfloat16 [16384, 4096], P('seq', 'head'), may hold values from -4 to 4
Outputs:
- mixed_out: bfloat16 [16384, 4096], P('seq', 'head')
- grad_queries: bfloat16 [16384, 32, 128], P('seq', 'head')
- grad_keys: bfloat16 [16384, 32, 128], P('seq', 'head')
- grad_values: bfloat16 [16384, 32, 128], P('seq', 'head')
- grad_levels: float32 [15, 32, 16384], P(None, 'head', 'seq')
All inputs are finite; a program needn't handle non-finite values.
Results may differ from a plain program's by a relative error of at most 0.017.
Values may be sent and summed in bfloat16 or wider, within the bound.
No kernel may reach another device: no remote copies, remote signals or barrier semaphores. Data moves between devices by JAX's collectives and lax.ppermute only.
A program may use at most 128 MiB of HBM per device.

v0:
```python
import jax
import jax.numpy as jnp
from jax import lax
from jax.sharding import PartitionSpec as P


def partner_2(block, axis, distance):
    count = lax.axis_size(axis)
    route = []
    for low in range(count):
        high = low | 1 << distance
        if high != low and high < count:
            route += [(low, high), (high, low)]
    return lax.ppermute(block, axis, route)


def in_blocks(array, dim, devices):
    before, after = (array.shape[:dim], array.shape[dim + 1 :])
    return jnp.moveaxis(array.reshape(*before, devices, -1, *after), dim, 0)


def summed_on_arrival(array, axis, dim):
    parts = in_blocks(array, dim, lax.axis_size(axis))
    arrived = lax.all_to_all(parts, axis, split_axis=0, concat_axis=0, tiled=True)
    return arrived.astype(jnp.float32).sum(axis=0)


def top_bit(differ, bit_total):
    count_bits = jnp.zeros(differ.shape, jnp.int32)
    for exponent in range(bit_total):
        count_bits = count_bits + (differ >= 2**exponent).astype(jnp.int32)
    return count_bits


def level_scales(level_total, head_width):
    raised = jnp.maximum(jnp.arange(level_total, dtype=jnp.int32) - 1, 0).astype(jnp.float32)
    return jnp.exp2(-0.5 * raised) / jnp.sqrt(jnp.float32(head_width))


def two_parts(exact_state):
    upper = exact_state.astype(jnp.bfloat16)
    lower = (exact_state - upper.astype(jnp.float32)).astype(jnp.bfloat16)
    return (upper, lower)


def state_first(form, exact_state, plain):
    upper, lower = two_parts(exact_state)
    return jnp.einsum(form, upper, plain, preferred_element_type=jnp.float32) + jnp.einsum(
        form, lower, plain, preferred_element_type=jnp.float32
    )


def state_second(form, plain, exact_state):
    upper, lower = two_parts(exact_state)
    return jnp.einsum(form, plain, upper, preferred_element_type=jnp.float32) + jnp.einsum(
        form, plain, lower, preferred_element_type=jnp.float32
    )


def on_device(queries, key_matrix, value_matrix, level_weight, out_weight, grad_out):
    rows_dev, head_count, head_width = queries.shape
    level_total = level_weight.shape[0]
    near_levels = rows_dev.bit_length()
    far_levels = lax.axis_size("seq").bit_length() - 1
    my_block = lax.axis_index("seq")
    scales = level_scales(level_total, head_width)
    weighted_levels = level_weight * scales[:, None, None]
    flat_out = out_weight.reshape(head_count * head_width, out_weight.shape[2])
    columns = flat_out
    mix_sum = lax.dot_general(
        lax.all_gather(grad_out, "head", axis=1, tiled=True),
        columns,
        (((1,), (1,)), ((), ())),
        preferred_element_type=jnp.float32,
    )
    grad_mix = mix_sum.astype(jnp.bfloat16).reshape(rows_dev, head_count, head_width)
    mix_f = grad_mix.astype(jnp.float32)
    key_weighted = jnp.einsum(
        "gpl,gpq->plq", key_matrix, value_matrix, preferred_element_type=jnp.float32
    )
    far_weights = weighted_levels[near_levels:]
    weighted = (
        far_weights[:, :, :, None] * jnp.transpose(queries.astype(jnp.float32), (1, 0, 2))[None]
    )
    back_states = state_first("jhik,ihv->jhkv", weighted, grad_mix)
    every = lax.all_gather(
        key_weighted[None].astype(jnp.bfloat16), "seq", axis=0, tiled=True
    ).astype(jnp.float32)
    block_ids = jnp.arange(every.shape[0], dtype=jnp.int32)
    block_gap = top_bit(jnp.bitwise_xor(block_ids, my_block), far_levels)
    level_ladder = jnp.arange(1, far_levels + 1, dtype=jnp.int32)
    masks = ((block_gap[None] == level_ladder[:, None]) & (block_ids < my_block)[None]).astype(
        jnp.float32
    )
    left_states = jnp.einsum("je,ehkv->jhkv", masks, every)
    pending = back_states
    right_list = []
    for bit_index in range(far_levels):
        partner = partner_2(pending.astype(jnp.bfloat16), "seq", bit_index).astype(pending.dtype)
        bit_off = 1.0 - (my_block // 2**bit_index % 2).astype(jnp.float32)
        right_list.append(bit_off * partner[0])
        pending = pending[1:] + partner[1:]
    right_states = jnp.stack(right_list)
    rows_index = lax.broadcasted_iota(jnp.int32, (rows_dev, near_levels, rows_dev), 0)
    tier_index = lax.broadcasted_iota(jnp.int32, (rows_dev, near_levels, rows_dev), 1)
    cols_index = lax.broadcasted_iota(jnp.int32, (rows_dev, near_levels, rows_dev), 2)
    near_gap = top_bit(jnp.bitwise_xor(rows_index, cols_index), near_levels - 1)
    onehot = ((near_gap == tier_index) & (cols_index <= rows_index)).astype(jnp.float32)
    mixing = jnp.einsum("ilj,lhi->hij", onehot, weighted_levels[:near_levels])
    scores = jnp.einsum("ihk,jhk->hij", queries, key_matrix, preferred_element_type=jnp.float32)
    attention = (scores * mixing).astype(jnp.bfloat16)
    local_out = jnp.einsum(
        "hij,jhv->ihv", attention, value_matrix, preferred_element_type=jnp.float32
    )
    far_rows = jnp.transpose(far_weights, (0, 2, 1))[..., None]
    reads = state_second("ihk,jhkv->jihv", queries, left_states)
    attended = (local_out + jnp.sum(far_rows * reads, axis=0)).astype(jnp.bfloat16)
    flat_att = attended.reshape(rows_dev, head_count * head_width)
    columns = flat_out
    mixed_cols = summed_on_arrival(
        lax.dot_general(
            columns, flat_att, (((0,), (1,)), ((), ())), preferred_element_type=jnp.float32
        ).astype(jnp.bfloat16),
        "head",
        0,
    )
    mixed_out = jnp.transpose(mixed_cols).astype(jnp.bfloat16)
    back = jnp.einsum("ihv,jhv->hij", grad_mix, value_matrix, preferred_element_type=jnp.float32)
    near_grad = jnp.einsum("ilj,hij->lhi", onehot, scores * back) * scales[:near_levels, None, None]
    far_grad = (
        jnp.transpose(jnp.sum(reads * mix_f[None], axis=3), (0, 2, 1))
        * scales[near_levels:, None, None]
    )
    grad_score = (back * mixing).astype(jnp.bfloat16)
    grad_queries = jnp.einsum(
        "hij,jhk->ihk", grad_score, key_matrix, preferred_element_type=jnp.float32
    )
    grad_queries = grad_queries + jnp.sum(
        far_rows * state_first("jhkv,ihv->jihk", left_states, grad_mix), axis=0
    )
    grad_keys = jnp.einsum("hij,ihk->jhk", grad_score, queries, preferred_element_type=jnp.float32)
    grad_keys = grad_keys + state_first("jhkv,ihv->ihk", right_states, value_matrix)
    grad_values = jnp.einsum(
        "hij,ihv->jhv", attention, grad_mix, preferred_element_type=jnp.float32
    )
    grad_values = grad_values + state_first("jhkv,ihk->ihv", right_states, key_matrix)
    grad_levels = jnp.concatenate([near_grad, far_grad], 0)
    return (
        mixed_out,
        grad_queries.astype(jnp.bfloat16),
        grad_keys.astype(jnp.bfloat16),
        grad_values.astype(jnp.bfloat16),
        grad_levels,
    )


def solution(mesh):
    in_specs = (
        P("seq", "head", None),
        P("seq", "head", None),
        P("seq", "head", None),
        P(None, "head", "seq"),
        P("head", None, None),
        P("seq", "head"),
    )
    out_specs = (
        P("seq", "head"),
        P("seq", "head", None),
        P("seq", "head", None),
        P("seq", "head", None),
        P(None, "head", "seq"),
    )
    return jax.shard_map(
        on_device, mesh=mesh, in_specs=in_specs, out_specs=out_specs, check_vma=False
    )
```

profile of v0, /device:TPU:1, one launch (start us, length us, event | category | flops | bytes accessed | tf_op | source)
XLA Modules:
  0.0 221.7 jit_solution(6458625137675124422)
XLA Ops:
  8.2 2.0 convolution_convert_fusion.1
  11.5 3.9 %fusion.66 = f32[4,512,512]{2,1,0:T(8,128)} fusion(bf16[512,4,128]{2,1,0:T(4,128)(2,1)} %param.6, bf16[512,4,128]{2,1,0:T(4,128)(2,1)} %param.7), kind=kOutput, calls=%fused_computation.80 | convolution fusion | flops 268435456 | bytes 5242880 | tf_op jit(solution)/shard_map/ihk,jhk->hij/dot_general | solution.py:110
  16.8 12.6 %fusion.12 = f32[512,4,512]{2,1,0:T(4,128)} fusion(bf16[10,4,512]{0,1,2:T(4,128)(2,1)S(1)} %copy.141), kind=kOutput, calls=%fused_computation.15 | convolution fusion | flops 99614720 | bytes 4235264 | tf_op jit(solution)/shard_map/ilj,lhi->hij/dot_general | solution.py:109
  29.4 19.3 %all-gather.4.cloned.1.call-done = bf16[512,4096]{1,0:T(8,128)(2,1)} async-done(((bf16[512,512]{1,0:T(8,128)(2,1)}), bf16[512,4096]{1,0:T(8,128)(2,1)}) %all-gather.4.cloned.1.call-update) | async-done | bytes 4194320 | tf_op jit(solution)/shard_map/all_gather | solution.py:71
  48.7 7.0 %bitcast_convert_fusion.1 = (f32[512,4,128]{0,2,1:T(8,128)}, bf16[512,512]{0,1:T(8,128)(2,1)S(1)}) fusion(bf16[512,4096]{1,0:T(8,128)(2,1)} %all-gather.4.cloned.1.call-done, bf16[512,4096]{1,0:T(8,128)(2,1)} %bitcast.112), kind=kOutput, calls=%fused_computation.127 | convolution fusion | flops 2148007936 | bytes 9961472 | tf_op jit(solution)/shard_map/dot_general | solution.py:70
  55.6 2.4 %fusion.23 = f32[4,128,5,128]{3,1,2,0:T(8,128)S(1)} fusion(bf16[512,4,128,1]{0,2,3,1:T(8,128)(2,1)S(1)} %bitcast.102, f32[4,512,128]{2,1,0:T(8,128)S(1)} %copy.169, f32[5,4,512]{2,0,1:T(8,128)S(1)} %copy.168), kind=kOutput, calls=%fused_computation.33 | convolution fusion | flops 338165760 | bytes 2924544 | tf_op jit(solution)/shard_map/jhik,ihv->jhkv/dot_general | solution.py:48
  58.0 3.4 %fusion.119 = (bf16[5,4,128,128]{2,3,0,1:T(8,128)(2,1)}, f32[5,4,128,128]{2,3,0,1:T(8,128)}) fusion(f32[4,128,5,128]{3,1,2,0:T(8,128)S(1)} %fusion.23, bf16[512,4,128,1]{0,2,3,1:T(8,128)(2,1)S(1)} %bitcast.103, f32[4,512,128]{2,1,0:T(8,128)S(1)} %copy.169, f32[5,4,512]{2,0,1:T(8,128)S(1)} %copy.168), kind=kOutput, calls=%fused_computation.151 | convolution fusion | flops 342753280 | bytes 4890624 | tf_op jit(solution)/shard_map/jhik,ihv->jhkv/dot_general | solution.py:48
  62.7 3.5 %fusion.19 = (bf16[4,512,512]{2,1,0:T(8,128)(2,1)S(1)}, bf16[4,512,512]{2,1,0:T(8,128)(2,1)}, f32[4,512,512]{2,1,0:T(8,128)S(1)}) fusion(f32[512,4,512]{2,1,0:T(4,128)S(1)} %copy-done.10, f32[4,512,512]{2,1,0:T(8,128)S(1)} %copy-done.1, bf16[512,4,128]{0,2,1:T(8,128)(2,1)S(1)} %bitcast.104, bf16[512,4,128]{2,1,0:T(4,128)(2,1)S(1)} %copy-done), kind=kOutput, calls=%fused_computation.29 | convolution fusion | flops 272629760 | bytes 17825792 | tf_op jit(solution)/shard_map/ihv,jhv->hij/dot_general | solution.py:128
  67.4 13.1 %fusion.47 = f32[10,4,512]{0,1,2:T(4,128)} fusion(bf16[4,512,512]{2,1,0:T(8,128)(2,1)S(1)} %mul.130, f32[10]{0:T(128)S(1)} %bitcast.111), kind=kOutput, calls=%fused_computation.58 | convolution fusion | flops 99635200 | bytes 2179112 | tf_op jit(solution)/shard_map/ilj,hij->lhi/dot_general | solution.py:129
  80.5 1.5 copy.179
  82.0 1.9 convolution_bitcast_fusion
  83.9 2.5 %fusion.120 = f32[4,128,512]{2,1,0:T(8,128)} fusion(bf16[512,4,128]{0,2,1:T(8,128)(2,1)} %bitcast.105, bf16[4,512,512]{2,1,0:T(8,128)(2,1)S(1)} %copy-done.5), kind=kOutput, calls=%fused_computation.152 | convolution fusion | flops 268435456 | bytes 3670016 | tf_op jit(solution)/shard_map/hij,ihv->jhv/dot_general | solution.py:143
  87.7 1.3 fusion.117
  89.0 2.5 %collective-permute-start.1 = (bf16[4,4,128,128]{2,3,0,1:T(8,128)(2,1)}, bf16[4,4,128,128]{2,3,0,1:T(8,128)(2,1)}, u32[]{:S(2)}, u32[]{:S(2)}) collective-permute-start(bf16[4,4,128,128]{2,3,0,1:T(8,128)(2,1)} %get-tuple-element.33), channel_id=1, source_target_pairs={{0,16},{16,0},{8,24},{24,8},{32,48},{48,32},{40,56},{56,40},{64,80... | collective-permute-start | bytes 1572872 | tf_op jit(solution)/shard_map/ppermute | solution.py:14
  92.2 38.1 %all-gather.6.cloned.1.call-done = bf16[128,128,128]{2,1,0:T(8,128)(2,1)} async-done(((bf16[4,128,128]{2,1,0:T(8,128)(2,1)}), bf16[128,128,128]{2,1,0:T(8,128)(2,1)}) %all-gather.6.cloned.1.call-update) | async-done | bytes 4194320 | tf_op jit(solution)/shard_map/all_gather | solution.py:86
  130.3 4.5 %fusion.21 = f32[5,4,128,128]{3,0,2,1:T(8,128)S(1)} fusion(bf16[32,4,128,128]{3,2,1,0:T(8,128)(2,1)} %bitcast.108, s32[32]{0:T(128)S(1)} %fusion.96, s32[5]{0:T(128)S(1)} %iota_add_fusion, pred[32]{0:T(512)(128)(4,1)S(1)} %iota_compare_fusion.2), kind=kOutput, calls=%fused_computation.31 | convolution fusion | flops 20971840 | bytes 5505204 | tf_op jit(solution)/shard_map/je,ehkv->jhkv/dot_general | solution.py:95
  137.2 2.6 %fusion.17 = (f32[5,512,4]{1,0,2:T(8,128)S(1)}, f32[512,4,128]{0,2,1:T(8,128)}) fusion(f32[512,4,128]{0,2,1:T(8,128)S(1)} %copy-done.17, f32[5,512,4]{1,0,2:T(8,128)S(1)} %copy.144, f32[4,5,128,512]{3,2,1,0:T(8,128)S(1)} %fusion.61, bf16[512,4,128,1]{2,1,0,3:T(4,128)(2,1)S(1)} %bitcast.101, bf16[5,4,128,128]{3,2,1,0:T(8,128)(2,1)S(1)} %subtract_convert_fusion), kind=kOutput, calls=%fused_computation.24 | convolution fusion | flops 341825536 | bytes 8601600 | tf_op jit(solution)/shard_map/ihk,jhkv->jihv/dot_general | solution.py:55
  139.8 2.5 %copy.154 = f32[512,4,128]{2,0,1:T(8,128)} copy(f32[512,4,128]{0,2,1:T(8,128)} %get-tuple-element.26) | data formatting | bytes 2097152 | tf_op jit(solution)/shard_map/reduce_sum | solution.py:117
  142.3 7.1 %bitcast_convert_fusion = bf16[512,4096]{1,0:T(8,128)(2,1)} fusion(bf16[4,128,4096]{2,1,0:T(8,128)(2,1)} %param.10, f32[512,4,128]{2,0,1:T(8,128)} %copy.154, bf16[4,512,512]{2,1,0:T(8,128)(2,1)} %get-tuple-element.36, bf16[512,4,128]{2,1,0:T(4,128)(2,1)S(1)} %copy-done), kind=kOutput, calls=%fused_computation.13 | convolution fusion | flops 2418540544 | bytes 12058624 | tf_op jit(solution)/shard_map/dot_general | solution.py:121
  149.5 4.5 %copy.270 = bf16[64,8,8,512]{3,2,0,1:T(8,128)(2,1)} copy(bf16[64,8,8,512]{3,2,1,0:T(8,128)(2,1)} %bitcast.109) | data formatting | bytes 8388608 | tf_op jit(solution)/shard_map/reshape | solution.py:19
  154.0 8.3 %all-to-all-start = ((bf16[8,512,512]{1,2,0:T(8,128)(2,1)}), bf16[8,512,512]{1,2,0:T(8,128)(2,1)}, u32[]{:S(2)}, u32[]{:S(2)}) async-start(bf16[8,512,512]{1,2,0:T(8,128)(2,1)} %bitcast.99), calls=%async_computation | async-start | bytes 8388608 | tf_op jit(solution)/shard_map/all_to_all | solution.py:24
  162.3 2.0 fusion.59
  168.8 1.9 fusion.15
  170.7 2.7 %copy.165 = f32[512,4,128]{2,0,1:T(8,128)} copy(f32[512,4,128]{0,2,1:T(8,128)} %fusion.15) | data formatting | bytes 2097152 | tf_op jit(solution)/shard_map/reduce_sum | solution.py:138
  173.4 2.2 fusion.54
  175.6 2.9 %collective-permute-done.2 = bf16[3,4,128,128]{2,3,0,1:T(8,128)(2,1)} collective-permute-done((bf16[3,4,128,128]{2,3,0,1:T(8,128)(2,1)}, bf16[3,4,128,128]{2,3,0,1:T(8,128)(2,1)}, u32[]{:S(2)}, u32[]{:S(2)}) %collective-permute-start.2) | collective-permute-done | bytes 393248 | tf_op jit(solution)/shard_map/ppermute | solution.py:14
  179.6 1.9 collective-permute-start.3
  182.6 11.1 %collective-permute-done.3 = bf16[2,4,128,128]{2,3,0,1:T(8,128)(2,1)S(1)} collective-permute-done((bf16[2,4,128,128]{2,3,0,1:T(8,128)(2,1)S(1)}, bf16[2,4,128,128]{2,3,0,1:T(8,128)(2,1)S(1)}, u32[]{:S(2)}, u32[]{:S(2)}) %collective-permute-start.3) | collective-permute-done | bytes 262176 | tf_op jit(solution)/shard_map/ppermute | solution.py:14
  193.8 2.6 %collective-permute-start.4 = (bf16[1,4,128,128]{2,3,0,1:T(8,128)(2,1)S(1)}, bf16[1,4,128,128]{2,3,0,1:T(8,128)(2,1)S(1)}, u32[]{:S(2)}, u32[]{:S(2)}) collective-permute-start(bf16[1,4,128,128]{2,3,0,1:T(8,128)(2,1)S(1)} %get-tuple-element.37), channel_id=1, source_target_pairs={{0,128},{128,0},{8,136},{136,8},{16,144},{144,16},{24,152},{152,24... | collective-permute-start | bytes 393224 | tf_op jit(solution)/shard_map/ppermute | solution.py:14
  198.3 6.2 %collective-permute-done.4 = bf16[1,4,128,128]{2,3,0,1:T(8,128)(2,1)S(1)} collective-permute-done((bf16[1,4,128,128]{2,3,0,1:T(8,128)(2,1)S(1)}, bf16[1,4,128,128]{2,3,0,1:T(8,128)(2,1)S(1)}, u32[]{:S(2)}, u32[]{:S(2)}) %collective-permute-start.4) | collective-permute-done | bytes 131104 | tf_op jit(solution)/shard_map/ppermute | solution.py:14
  208.3 2.8 %all-to-all-done = bf16[8,512,512]{1,2,0:T(8,128)(2,1)} async-done(((bf16[8,512,512]{1,2,0:T(8,128)(2,1)}), bf16[8,512,512]{1,2,0:T(8,128)(2,1)}, u32[]{:S(2)}, u32[]{:S(2)}) %all-to-all-start) | async-done | bytes 4194336 | tf_op jit(solution)/shard_map/all_to_all | solution.py:24
  211.1 3.7 %reduce_sum.66 = bf16[512,512]{0,1:T(8,128)(2,1)} reduce(bf16[8,512,512]{1,2,0:T(8,128)(2,1)} %all-to-all-done, bf16[]{:T(256)} %constant.118.clone.1), dimensions={0}, to_apply=%region_1.2 | reduce | flops 1835008 | bytes 4718594 | tf_op jit(solution)/shard_map/reduce_sum | solution.py:25
  (89 shorter events, 22.3 us)
Async XLA Ops:
  7.2 1.0 copy-start
  7.2 41.5 %all-gather.4.cloned.1.call-start = ((), (), s32[]{:S(2)}) async-start(), calls=%async_computation.1 | async-start | bytes 4718592 | tf_op jit(solution)/shard_map/all_gather | solution.py:71
  7.9 7.5 %copy-start.19 = (f32[15,4,512]{2,1,0:T(4,128)S(1)}, f32[15,4,512]{2,1,0:T(4,128)}, u32[]{:S(2)}) copy-start(f32[15,4,512]{2,1,0:T(4,128)} %param.9) | copy-start | bytes 368644
  7.9 122.4 %all-gather.6.cloned.1.call-start = ((), (), s32[]{:S(2)}) async-start(), calls=%async_computation.2 | async-start | bytes 4325376 | tf_op jit(solution)/shard_map/all_gather | solution.py:86
  48.7 14.0 %copy-start.10 = (f32[512,4,512]{2,1,0:T(4,128)S(1)}, f32[512,4,512]{2,1,0:T(4,128)}, u32[]{:S(2)}) copy-start(f32[512,4,512]{2,1,0:T(4,128)} %fusion.12) | copy-start | bytes 12582916
  55.6 10.5 %copy-start.3 = (bf16[512,512]{0,1:T(8,128)(2,1)}, bf16[512,512]{0,1:T(8,128)(2,1)S(1)}, u32[]{:S(2)}) copy-start(bf16[512,512]{0,1:T(8,128)(2,1)S(1)} %get-tuple-element.42) | copy-start | bytes 1572868
  55.6 7.0 %copy-start.1 = (f32[4,512,512]{2,1,0:T(8,128)S(1)}, f32[4,512,512]{2,1,0:T(8,128)}, u32[]{:S(2)}) copy-start(f32[4,512,512]{2,1,0:T(8,128)} %fusion.66) | copy-start | bytes 12582916
  61.4 25.0 %collective-permute-start = (bf16[5,4,128,128]{2,3,0,1:T(8,128)(2,1)}, bf16[5,4,128,128]{2,3,0,1:T(8,128)(2,1)}, u32[]{:S(2)}, u32[]{:S(2)}) collective-permute-start(bf16[5,4,128,128]{2,3,0,1:T(8,128)(2,1)} %get-tuple-element.44), channel_id=1, source_target_pairs={{0,8},{8,0},{16,24},{24,16},{32,40},{40,32},{48,56},{56,48},{64,72... | collective-permute-start | bytes 1966088 | tf_op jit(solution)/shard_map/ppermute | solution.py:14
  67.3 14.7 %copy-start.2 = (bf16[512,4,128]{2,1,0:T(4,128)(2,1)S(1)}, bf16[512,4,128]{2,1,0:T(4,128)(2,1)}, u32[]{:S(2)}) copy-start(bf16[512,4,128]{2,1,0:T(4,128)(2,1)} %param.6) | copy-start | bytes 1572868
  82.0 1.9 copy-start.5
  82.0 5.6 %copy-start.18 = (f32[5,4,128,128]{2,3,0,1:T(8,128)S(1)}, f32[5,4,128,128]{2,3,0,1:T(8,128)}, u32[]{:S(2)}) copy-start(f32[5,4,128,128]{2,3,0,1:T(8,128)} %get-tuple-element.45) | copy-start | bytes 3932164
  89.0 75.4 %collective-permute-start.1 = (bf16[4,4,128,128]{2,3,0,1:T(8,128)(2,1)}, bf16[4,4,128,128]{2,3,0,1:T(8,128)(2,1)}, u32[]{:S(2)}, u32[]{:S(2)}) collective-permute-start(bf16[4,4,128,128]{2,3,0,1:T(8,128)(2,1)} %get-tuple-element.33), channel_id=1, source_target_pairs={{0,16},{16,0},{8,24},{24,8},{32,48},{48,32},{40,56},{56,40},{64,80... | collective-permute-start | bytes 1572872 | tf_op jit(solution)/shard_map/ppermute | solution.py:14
  135.1 2.0 copy-start.7
  135.1 2.0 copy-start.17
  135.4 0.9 copy-start.9
  154.0 8.3 %copy-start.4 = (bf16[512,512]{0,1:T(8,128)(2,1)S(1)}, bf16[512,512]{0,1:T(8,128)(2,1)}, u32[]{:S(2)}) copy-start(bf16[512,512]{0,1:T(8,128)(2,1)} %copy-done.3) | copy-start | bytes 1572868
  154.0 57.1 %all-to-all-start = ((bf16[8,512,512]{1,2,0:T(8,128)(2,1)}), bf16[8,512,512]{1,2,0:T(8,128)(2,1)}, u32[]{:S(2)}, u32[]{:S(2)}) async-start(bf16[8,512,512]{1,2,0:T(8,128)(2,1)} %bitcast.99), calls=%async_computation | async-start | bytes 8388608 | tf_op jit(solution)/shard_map/all_to_all | solution.py:24
  162.3 4.2 %copy-start.14 = (f32[4,4,128,128]{2,3,0,1:T(8,128)S(1)}, f32[4,4,128,128]{2,3,0,1:T(8,128)}, u32[]{:S(2)}) copy-start(f32[4,4,128,128]{2,3,0,1:T(8,128)} %get-tuple-element.34) | copy-start | bytes 3145732
  162.3 6.5 %copy-start.8 = (bf16[5,4,128,128]{3,2,1,0:T(8,128)(2,1)S(1)}, bf16[5,4,128,128]{3,2,1,0:T(8,128)(2,1)}, u32[]{:S(2)}) copy-start(bf16[5,4,128,128]{3,2,1,0:T(8,128)(2,1)} %copy-done.7) | copy-start | bytes 1966084
  165.5 1.0 copy-start.13
  167.6 10.8 %collective-permute-start.2 = (bf16[3,4,128,128]{2,3,0,1:T(8,128)(2,1)}, bf16[3,4,128,128]{2,3,0,1:T(8,128)(2,1)}, u32[]{:S(2)}, u32[]{:S(2)}) collective-permute-start(bf16[3,4,128,128]{2,3,0,1:T(8,128)(2,1)} %get-tuple-element.31), channel_id=1, source_target_pairs={{0,32},{32,0},{8,40},{40,8},{16,48},{48,16},{24,56},{56,24},{64,96... | collective-permute-start | bytes 1179656 | tf_op jit(solution)/shard_map/ppermute | solution.py:14
  170.7 8.9 %copy-start.15 = (f32[3,4,128,128]{2,3,0,1:T(8,128)S(1)}, f32[3,4,128,128]{2,3,0,1:T(8,128)}, u32[]{:S(2)}) copy-start(f32[3,4,128,128]{2,3,0,1:T(8,128)} %get-tuple-element.32) | copy-start | bytes 2359300
  173.4 8.2 %copy-start.16 = (f32[5,4,128,128]{2,3,0,1:T(8,128)S(1)}, f32[5,4,128,128]{2,3,0,1:T(8,128)}, u32[]{:S(2)}) copy-start(f32[5,4,128,128]{2,3,0,1:T(8,128)} %fusion.86) | copy-start | bytes 3932164
  173.4 23.0 %copy-start.20 = (f32[5]{0:T(128)S(1)}, f32[5]{0:T(128)}, u32[]{:S(2)}) copy-start(f32[5]{0:T(128)} %slice.63) | copy-start | bytes 64
  179.6 25.4 %copy-start.12 = (f32[512,4,128]{2,0,1:T(8,128)S(1)}, f32[512,4,128]{2,0,1:T(8,128)}, u32[]{:S(2)}) copy-start(f32[512,4,128]{2,0,1:T(8,128)} %convolution_bitcast_fusion) | copy-start | bytes 3145732
  179.6 14.0 %collective-permute-start.3 = (bf16[2,4,128,128]{2,3,0,1:T(8,128)(2,1)S(1)}, bf16[2,4,128,128]{2,3,0,1:T(8,128)(2,1)S(1)}, u32[]{:S(2)}, u32[]{:S(2)}) collective-permute-start(bf16[2,4,128,128]{2,3,0,1:T(8,128)(2,1)S(1)} %get-tuple-element.29), channel_id=1, source_target_pairs={{0,64},{64,0},{8,72},{72,8},{16,80},{80,16},{24,88},{88,24},{32,96... | collective-permute-start | bytes 786440 | tf_op jit(solution)/shard_map/ppermute | solution.py:14
  193.8 10.8 %collective-permute-start.4 = (bf16[1,4,128,128]{2,3,0,1:T(8,128)(2,1)S(1)}, bf16[1,4,128,128]{2,3,0,1:T(8,128)(2,1)S(1)}, u32[]{:S(2)}, u32[]{:S(2)}) collective-permute-start(bf16[1,4,128,128]{2,3,0,1:T(8,128)(2,1)S(1)} %get-tuple-element.37), channel_id=1, source_target_pairs={{0,128},{128,0},{8,136},{136,8},{16,144},{144,16},{24,152},{152,24... | collective-permute-start | bytes 393224 | tf_op jit(solution)/shard_map/ppermute | solution.py:14
  197.6 8.9 %copy-start.6 = (bf16[512,4,128]{2,1,0:T(4,128)(2,1)S(1)}, bf16[512,4,128]{2,1,0:T(4,128)(2,1)}, u32[]{:S(2)}) copy-start(bf16[512,4,128]{2,1,0:T(4,128)(2,1)} %param.7) | copy-start | bytes 1572868
  204.7 2.1 copy-start.11
Sparse Core Ops, SparseCore 0:
  9.8 38.7 all-gather.3
  51.8 78.4 all-gather.5
where the time goes:
time: 222 us
  waiting for transfers between devices  81.1 us (37%)
  matrix products  74.8 us (34%)
  local copies, waits for them, and re-layouts  18.3 us (8%)
  starting transfers between devices  17.7 us (8%)
  other arithmetic  15.1 us (7%)
  between operations  14.6 us (7%)
    all_gather x1, waiting for transfers between devices, on_device(): lax.all_gather(key_weighted[None].astype(jnp.bfloat16), 'seq', axis=0, ti...  38.1 us
    ppermute x5, waiting for transfers between devices, partner_2(): return lax.ppermute(block, axis, route)  20.2 us
    all_gather x1, waiting for transfers between devices, on_device(): lax.all_gather(grad_out, 'head', axis=1, tiled=True)  19.3 us
    dot_general x1, matrix products, on_device(): jnp.einsum('ilj,hij->lhi', onehot, scores * back)  13.1 us
    dot_general x1, matrix products, on_device(): mixing = jnp.einsum('ilj,lhi->hij', onehot, weighted_levels[:near_levels])  12.6 us
    ppermute x5, starting transfers between devices, partner_2(): return lax.ppermute(block, axis, route)  9.37 us
    all_to_all x1, starting transfers between devices, summed_on_arrival(): lax.all_to_all(parts, axis, split_axis=0, concat_axis=0, tiled=True)  8.28 us
    dot_general x1, matrix products, on_device(): lax.dot_general(columns, flat_att, (((0,), (1,)), ((), ())), preferred_el...  7.13 us
  transfers between devices with their start and end apart: 8, of which 6 were waited for; matrix products, arithmetic and copies ran while one was open for 46% of the time, Pallas kernels for 0%

commit v1 on v0

--- a/solution.py
+++ b/solution.py
@@ -2,6 +2,11 @@
 import jax.numpy as jnp
 from jax import lax
 from jax.sharding import PartitionSpec as P
+
+
+def tiled_gather(array, axis, dim):
+    copies = jnp.concatenate([array] * lax.axis_size(axis), axis=dim)
+    return lax.all_to_all(copies, axis, dim, dim, tiled=True)
 
 
 def partner_2(block, axis, distance):
@@ -83,9 +88,7 @@
         far_weights[:, :, :, None] * jnp.transpose(queries.astype(jnp.float32), (1, 0, 2))[None]
     )
     back_states = state_first("jhik,ihv->jhkv", weighted, grad_mix)
-    every = lax.all_gather(
-        key_weighted[None].astype(jnp.bfloat16), "seq", axis=0, tiled=True
-    ).astype(jnp.float32)
+    every = tiled_gather(key_weighted[None].astype(jnp.bfloat16), "seq", 0).astype(jnp.float32)
     block_ids = jnp.arange(every.shape[0], dtype=jnp.int32)
     block_gap = top_bit(jnp.bitwise_xor(block_ids, my_block), far_levels)
     level_ladder = jnp.arange(1, far_levels + 1, dtype=jnp.int32)

time: 222 us -> 210 us (0.946)
  waiting for transfers between devices: 81.1 us -> 56.3 us
  starting transfers between devices: 17.7 us -> 28.3 us
  local copies, waits for them, and re-layouts: 18.3 us -> 21.8 us
    all_gather x1 -> x0, waiting for transfers between devices: 38.1 us -> none  [on_device(): lax.all_gather(key_weighted[None].astype(jnp.bfloat16), 'seq', axis=0, ti...]
    all_to_all x0 -> x1, waiting for transfers between devices: none -> 25.2 us  [tiled_gather(): return lax.all_to_all(copies, axis, dim, dim, tiled=True)]
    all_gather x1, waiting for transfers between devices: 19.3 us -> 6.51 us  [on_device(): lax.all_gather(grad_out, 'head', axis=1, tiled=True)]
    all_to_all x0 -> x1, starting transfers between devices: none -> 12.3 us  [tiled_gather(): return lax.all_to_all(copies, axis, dim, dim, tiled=True)]
    concatenate x0 -> x1, local copies, waits for them, and re-layouts: none -> 3.07 us  [tiled_gather(): copies = jnp.concatenate([array] * lax.axis_size(axis), axis=dim)]
    unnamed x45 -> x47, local copies, waits for them, and re-layouts: 5.61 us -> 5.64 us
  transfers between devices with their start and end apart: 8 -> 8, of which waited for: 6 -> 6; matrix products, arithmetic and copies ran while one was open for 46% -> 49% of each run, Pallas kernels for 0% -> 0%
where the time goes in v1:
time: 210 us; the launch traced here: 208 us
  matrix products  72.9 us (35%)
  waiting for transfers between devices  56.3 us (27%)
  starting transfers between devices  28.3 us (13%)
  local copies, waits for them, and re-layouts  21.8 us (10%)
  between operations  14.5 us (7%)
  other arithmetic  14.1 us (7%)
    all_to_all x1, waiting for transfers between devices, tiled_gather(): return lax.all_to_all(copies, axis, dim, dim, tiled=True)  25.2 us
    ppermute x5, waiting for transfers between devices, partner_2(): return lax.ppermute(block, axis, route)  21.1 us
    dot_general x1, matrix products, on_device(): jnp.einsum('ilj,hij->lhi', onehot, scores * back)  13.1 us
    dot_general x1, matrix products, on_device(): mixing = jnp.einsum('ilj,lhi->hij', onehot, weighted_levels[:near_levels])  12.5 us
    all_to_all x1, starting transfers between devices, tiled_gather(): return lax.all_to_all(copies, axis, dim, dim, tiled=True)  12.3 us
    ppermute x5, starting transfers between devices, partner_2(): return lax.ppermute(block, axis, route)  9.23 us
    dot_general x1, matrix products, on_device(): lax.dot_general(columns, flat_att, (((0,), (1,)), ((), ())), preferred_el...  7.13 us
    dot_general x1, matrix products, on_device(): lax.dot_general(lax.all_gather(grad_out, 'head', axis=1, tiled=True), col...  6.96 us
  transfers between devices with their start and end apart: 8, of which 6 were waited for; matrix products, arithmetic and copies ran while one was open for 49% of the time, Pallas kernels for 0%

profile of v1, /device:TPU:1, one launch (start us, length us, event | category | flops | bytes accessed | tf_op | source)
XLA Modules:
  0.0 207.8 jit_solution(5078401765017260268)
XLA Ops:
  9.6 3.1 %concatenate.6 = bf16[32,4,128,128]{3,2,1,0:T(8,128)(2,1)} broadcast(bf16[4,128,128]{2,1,0:T(8,128)(2,1)S(1)} %convolution_convert_fusion.1), dimensions={1,2,3} | broadcast | bytes 4325376 | tf_op jit(solution)/shard_map/concatenate | solution.py:8
  12.7 12.3 %all-to-all-start = ((bf16[32,4,128,128]{3,2,1,0:T(8,128)(2,1)}), bf16[32,4,128,128]{3,2,1,0:T(8,128)(2,1)}, u32[]{:S(2)}, u32[]{:S(2)}) async-start(bf16[32,4,128,128]{3,2,1,0:T(8,128)(2,1)} %concatenate.6), calls=%async_computation | async-start | bytes 8388608 | tf_op jit(solution)/shard_map/all_to_all | solution.py:9
  25.3 2.7 %fusion.66 = f32[4,512,512]{2,1,0:T(8,128)} fusion(bf16[512,4,128]{2,1,0:T(4,128)(2,1)S(1)} %copy-done.2, bf16[512,4,128]{2,1,0:T(4,128)(2,1)S(1)} %copy-done.6), kind=kOutput, calls=%fused_computation.80 | convolution fusion | flops 268435456 | bytes 5242880 | tf_op jit(solution)/shard_map/ihk,jhk->hij/dot_general | solution.py:113
  29.6 12.5 %fusion.12 = f32[512,4,512]{2,1,0:T(4,128)} fusion(bf16[10,4,512]{0,1,2:T(4,128)(2,1)S(1)} %copy.92), kind=kOutput, calls=%fused_computation.15 | convolution fusion | flops 99614720 | bytes 4235264 | tf_op jit(solution)/shard_map/ilj,lhi->hij/dot_general | solution.py:112
  42.1 6.5 %all-gather.2.cloned.1.call-done = bf16[512,4096]{1,0:T(8,128)(2,1)} async-done(((bf16[512,512]{1,0:T(8,128)(2,1)}), bf16[512,4096]{1,0:T(8,128)(2,1)}) %all-gather.2.cloned.1.call-update) | async-done | bytes 4194320 | tf_op jit(solution)/shard_map/all_gather | solution.py:76
  48.6 7.0 %bitcast_convert_fusion.1 = (f32[512,4,128]{0,2,1:T(8,128)}, bf16[512,512]{0,1:T(8,128)(2,1)S(1)}) fusion(bf16[512,4096]{1,0:T(8,128)(2,1)} %all-gather.2.cloned.1.call-done, bf16[512,4096]{1,0:T(8,128)(2,1)} %bitcast.110), kind=kOutput, calls=%fused_computation.127 | convolution fusion | flops 2148007936 | bytes 9961472 | tf_op jit(solution)/shard_map/dot_general | solution.py:75
  55.6 2.4 %fusion.23 = f32[4,128,5,128]{3,1,2,0:T(8,128)S(1)} fusion(bf16[512,4,128,1]{0,2,3,1:T(8,128)(2,1)S(1)} %bitcast.101, f32[4,512,128]{2,1,0:T(8,128)S(1)} %copy-done.19, f32[5,4,512]{2,0,1:T(8,128)S(1)} %copy.119), kind=kOutput, calls=%fused_computation.33 | convolution fusion | flops 338165760 | bytes 2924544 | tf_op jit(solution)/shard_map/jhik,ihv->jhkv/dot_general | solution.py:53
  58.0 3.4 %fusion.119 = (bf16[5,4,128,128]{2,3,0,1:T(8,128)(2,1)}, f32[5,4,128,128]{2,3,0,1:T(8,128)}) fusion(f32[4,128,5,128]{3,1,2,0:T(8,128)S(1)} %fusion.23, bf16[512,4,128,1]{0,2,3,1:T(8,128)(2,1)S(1)} %bitcast.102, f32[4,512,128]{2,1,0:T(8,128)S(1)} %copy-done.19, f32[5,4,512]{2,0,1:T(8,128)S(1)} %copy.119), kind=kOutput, calls=%fused_computation.151 | convolution fusion | flops 342753280 | bytes 4890624 | tf_op jit(solution)/shard_map/jhik,ihv->jhkv/dot_general | solution.py:53
  62.6 3.5 %fusion.19 = (bf16[4,512,512]{2,1,0:T(8,128)(2,1)S(1)}, bf16[4,512,512]{2,1,0:T(8,128)(2,1)}, f32[4,512,512]{2,1,0:T(8,128)S(1)}) fusion(f32[512,4,512]{2,1,0:T(4,128)S(1)} %copy-done.11, f32[4,512,512]{2,1,0:T(8,128)S(1)} %copy-done.1, bf16[512,4,128]{0,2,1:T(8,128)(2,1)S(1)} %bitcast.103, bf16[512,4,128]{2,1,0:T(4,128)(2,1)S(1)} %copy-done), kind=kOutput, calls=%fused_computation.29 | convolution fusion | flops 272629760 | bytes 17825792 | tf_op jit(solution)/shard_map/ihv,jhv->hij/dot_general | solution.py:131
  67.3 13.1 %fusion.47 = f32[10,4,512]{0,1,2:T(4,128)} fusion(bf16[4,512,512]{2,1,0:T(8,128)(2,1)S(1)} %mul.130, f32[10]{0:T(128)S(1)} %bitcast.109), kind=kOutput, calls=%fused_computation.58 | convolution fusion | flops 99635200 | bytes 2179112 | tf_op jit(solution)/shard_map/ilj,hij->lhi/dot_general | solution.py:132
  80.4 1.5 copy.130
  82.0 1.9 convolution_bitcast_fusion
  83.9 2.5 %fusion.120 = f32[4,128,512]{2,1,0:T(8,128)} fusion(bf16[512,4,128]{0,2,1:T(8,128)(2,1)} %bitcast.104, bf16[4,512,512]{2,1,0:T(8,128)(2,1)S(1)} %copy-done.5), kind=kOutput, calls=%fused_computation.152 | convolution fusion | flops 268435456 | bytes 3670016 | tf_op jit(solution)/shard_map/hij,ihv->jhv/dot_general | solution.py:146
  88.9 3.2 %collective-permute-start.1 = (bf16[4,4,128,128]{2,3,0,1:T(8,128)(2,1)}, bf16[4,4,128,128]{2,3,0,1:T(8,128)(2,1)}, u32[]{:S(2)}, u32[]{:S(2)}) collective-permute-start(bf16[4,4,128,128]{2,3,0,1:T(8,128)(2,1)} %get-tuple-element.28), channel_id=1, source_target_pairs={{0,16},{16,0},{8,24},{24,8},{32,48},{48,32},{40,56},{56,40},{64,80... | collective-permute-start | bytes 1572872 | tf_op jit(solution)/shard_map/ppermute | solution.py:19
  92.8 25.2 %all-to-all-done = bf16[32,4,128,128]{3,2,1,0:T(8,128)(2,1)} async-done(((bf16[32,4,128,128]{3,2,1,0:T(8,128)(2,1)}), bf16[32,4,128,128]{3,2,1,0:T(8,128)(2,1)}, u32[]{:S(2)}, u32[]{:S(2)}) %all-to-all-start) | async-done | bytes 4194336 | tf_op jit(solution)/shard_map/all_to_all | solution.py:9
  118.0 4.5 %fusion.21 = f32[5,4,128,128]{3,0,2,1:T(8,128)S(1)} fusion(bf16[32,4,128,128]{3,2,1,0:T(8,128)(2,1)} %all-to-all-done, s32[32]{0:T(128)S(1)} %fusion.96, s32[5]{0:T(128)S(1)} %iota_add_fusion, pred[32]{0:T(512)(128)(4,1)S(1)} %iota_compare_fusion.2), kind=kOutput, calls=%fused_computation.31 | convolution fusion | flops 20971840 | bytes 5505204 | tf_op jit(solution)/shard_map/je,ehkv->jhkv/dot_general | solution.py:98
  124.9 2.6 %fusion.17 = (f32[5,512,4]{1,0,2:T(8,128)S(1)}, f32[512,4,128]{0,2,1:T(8,128)}) fusion(f32[512,4,128]{0,2,1:T(8,128)S(1)} %copy-done.18, f32[5,512,4]{1,0,2:T(8,128)S(1)} %copy.95, f32[4,5,128,512]{3,2,1,0:T(8,128)S(1)} %fusion.61, bf16[512,4,128,1]{2,1,0,3:T(4,128)(2,1)S(1)} %bitcast.100, bf16[5,4,128,128]{3,2,1,0:T(8,128)(2,1)S(1)} %subtract_convert_fusion), kind=kOutput, calls=%fused_computation.24 | convolution fusion | flops 341825536 | bytes 8601600 | tf_op jit(solution)/shard_map/ihk,jhkv->jihv/dot_general | solution.py:60
  127.5 2.5 %copy.105 = f32[512,4,128]{2,0,1:T(8,128)} copy(f32[512,4,128]{0,2,1:T(8,128)} %get-tuple-element.21) | data formatting | bytes 2097152 | tf_op jit(solution)/shard_map/reduce_sum | solution.py:120
  130.0 7.1 %bitcast_convert_fusion = bf16[512,4096]{1,0:T(8,128)(2,1)} fusion(bf16[4,128,4096]{2,1,0:T(8,128)(2,1)} %param.10, f32[512,4,128]{2,0,1:T(8,128)} %copy.105, bf16[4,512,512]{2,1,0:T(8,128)(2,1)} %get-tuple-element.31, bf16[512,4,128]{2,1,0:T(4,128)(2,1)S(1)} %copy-done), kind=kOutput, calls=%fused_computation.13 | convolution fusion | flops 2418540544 | bytes 12058624 | tf_op jit(solution)/shard_map/dot_general | solution.py:124
  137.1 4.5 %copy.221 = bf16[64,8,8,512]{3,2,0,1:T(8,128)(2,1)} copy(bf16[64,8,8,512]{3,2,1,0:T(8,128)(2,1)} %bitcast.107) | data formatting | bytes 8388608 | tf_op jit(solution)/shard_map/reshape | solution.py:24
  141.7 6.8 %all-to-all-start.1 = ((bf16[8,512,512]{1,2,0:T(8,128)(2,1)}), bf16[8,512,512]{1,2,0:T(8,128)(2,1)}, u32[]{:S(2)}, u32[]{:S(2)}) async-start(bf16[8,512,512]{1,2,0:T(8,128)(2,1)} %bitcast.98), calls=%async_computation.1 | async-start | bytes 8388608 | tf_op jit(solution)/shard_map/all_to_all | solution.py:29
  148.4 2.0 fusion.59
  153.8 1.8 collective-permute-start.2
  155.6 1.9 fusion.15
  157.5 2.6 %copy.116 = f32[512,4,128]{2,0,1:T(8,128)} copy(f32[512,4,128]{0,2,1:T(8,128)} %fusion.15) | data formatting | bytes 2097152 | tf_op jit(solution)/shard_map/reduce_sum | solution.py:141
  160.1 2.2 %fusion.54 = bf16[512,4,128]{2,0,1:T(8,128)(2,1)S(1)} fusion(f32[512,4,128]{2,0,1:T(8,128)} %copy.116, bf16[4,512,512]{2,1,0:T(8,128)(2,1)S(1)} %get-tuple-element.30, bf16[512,4,128]{2,1,0:T(4,128)(2,1)} %param.7), kind=kOutput, calls=%fused_computation.62 | convolution fusion | flops 268959744 | bytes 4194304 | tf_op jit(solution)/shard_map/hij,jhk->ihk/dot_general | solution.py:138
  162.4 2.9 %collective-permute-done.2 = bf16[3,4,128,128]{2,3,0,1:T(8,128)(2,1)} collective-permute-done((bf16[3,4,128,128]{2,3,0,1:T(8,128)(2,1)}, bf16[3,4,128,128]{2,3,0,1:T(8,128)(2,1)}, u32[]{:S(2)}, u32[]{:S(2)}) %collective-permute-start.2) | collective-permute-done | bytes 393248 | tf_op jit(solution)/shard_map/ppermute | solution.py:19
  166.4 1.5 collective-permute-start.3
  169.0 11.5 %collective-permute-done.3 = bf16[2,4,128,128]{2,3,0,1:T(8,128)(2,1)S(1)} collective-permute-done((bf16[2,4,128,128]{2,3,0,1:T(8,128)(2,1)S(1)}, bf16[2,4,128,128]{2,3,0,1:T(8,128)(2,1)S(1)}, u32[]{:S(2)}, u32[]{:S(2)}) %collective-permute-start.3) | collective-permute-done | bytes 262176 | tf_op jit(solution)/shard_map/ppermute | solution.py:19
  184.1 6.7 %collective-permute-done.4 = bf16[1,4,128,128]{2,3,0,1:T(8,128)(2,1)S(1)} collective-permute-done((bf16[1,4,128,128]{2,3,0,1:T(8,128)(2,1)S(1)}, bf16[1,4,128,128]{2,3,0,1:T(8,128)(2,1)S(1)}, u32[]{:S(2)}, u32[]{:S(2)}) %collective-permute-start.4) | collective-permute-done | bytes 131104 | tf_op jit(solution)/shard_map/ppermute | solution.py:19
  194.5 2.8 %all-to-all-done.1 = bf16[8,512,512]{1,2,0:T(8,128)(2,1)} async-done(((bf16[8,512,512]{1,2,0:T(8,128)(2,1)}), bf16[8,512,512]{1,2,0:T(8,128)(2,1)}, u32[]{:S(2)}, u32[]{:S(2)}) %all-to-all-start.1) | async-done | bytes 4194336 | tf_op jit(solution)/shard_map/all_to_all | solution.py:29
  197.2 3.7 %reduce_sum.66 = bf16[512,512]{0,1:T(8,128)(2,1)} reduce(bf16[8,512,512]{1,2,0:T(8,128)(2,1)} %all-to-all-done.1, bf16[]{:T(256)} %constant.118.clone.1), dimensions={0}, to_apply=%region_1.2 | reduce | flops 1835008 | bytes 4718594 | tf_op jit(solution)/shard_map/reduce_sum | solution.py:30
  (91 shorter events, 24.7 us)
Async XLA Ops:
  7.2 1.0 copy-start
  7.2 41.4 %all-gather.2.cloned.1.call-start = ((), (), s32[]{:S(2)}) async-start(), calls=%async_computation.2 | async-start | bytes 4718592 | tf_op jit(solution)/shard_map/all_gather | solution.py:76
  12.7 12.3 %copy-start.21 = (f32[15,4,512]{2,1,0:T(4,128)S(1)}, f32[15,4,512]{2,1,0:T(4,128)}, u32[]{:S(2)}) copy-start(f32[15,4,512]{2,1,0:T(4,128)} %param.9) | copy-start | bytes 368644
  12.7 12.4 %copy-start.2 = (bf16[512,4,128]{2,1,0:T(4,128)(2,1)S(1)}, bf16[512,4,128]{2,1,0:T(4,128)(2,1)}, u32[]{:S(2)}) copy-start(bf16[512,4,128]{2,1,0:T(4,128)(2,1)} %param.6) | copy-start | bytes 1572868
  12.7 12.6 %copy-start.6 = (bf16[512,4,128]{2,1,0:T(4,128)(2,1)S(1)}, bf16[512,4,128]{2,1,0:T(4,128)(2,1)}, u32[]{:S(2)}) copy-start(bf16[512,4,128]{2,1,0:T(4,128)(2,1)} %param.7) | copy-start | bytes 1572868
  12.7 105.3 %all-to-all-start = ((bf16[32,4,128,128]{3,2,1,0:T(8,128)(2,1)}), bf16[32,4,128,128]{3,2,1,0:T(8,128)(2,1)}, u32[]{:S(2)}, u32[]{:S(2)}) async-start(bf16[32,4,128,128]{3,2,1,0:T(8,128)(2,1)} %concatenate.6), calls=%async_computation | async-start | bytes 8388608 | tf_op jit(solution)/shard_map/all_to_all | solution.py:9
  48.6 7.0 %copy-start.19 = (f32[4,512,128]{2,1,0:T(8,128)S(1)}, f32[4,512,128]{2,1,0:T(8,128)}, u32[]{:S(2)}) copy-start(f32[4,512,128]{2,1,0:T(8,128)} %copy.120) | copy-start | bytes 3145732
  48.6 14.0 %copy-start.11 = (f32[512,4,512]{2,1,0:T(4,128)S(1)}, f32[512,4,512]{2,1,0:T(4,128)}, u32[]{:S(2)}) copy-start(f32[512,4,512]{2,1,0:T(4,128)} %fusion.12) | copy-start | bytes 12582916
  55.6 10.5 %copy-start.3 = (bf16[512,512]{0,1:T(8,128)(2,1)}, bf16[512,512]{0,1:T(8,128)(2,1)S(1)}, u32[]{:S(2)}) copy-start(bf16[512,512]{0,1:T(8,128)(2,1)S(1)} %get-tuple-element.37) | copy-start | bytes 1572868
  55.6 7.0 %copy-start.1 = (f32[4,512,512]{2,1,0:T(8,128)S(1)}, f32[4,512,512]{2,1,0:T(8,128)}, u32[]{:S(2)}) copy-start(f32[4,512,512]{2,1,0:T(8,128)} %fusion.66) | copy-start | bytes 12582916
  61.4 24.9 %collective-permute-start = (bf16[5,4,128,128]{2,3,0,1:T(8,128)(2,1)}, bf16[5,4,128,128]{2,3,0,1:T(8,128)(2,1)}, u32[]{:S(2)}, u32[]{:S(2)}) collective-permute-start(bf16[5,4,128,128]{2,3,0,1:T(8,128)(2,1)} %get-tuple-element.39), channel_id=1, source_target_pairs={{0,8},{8,0},{16,24},{24,16},{32,40},{40,32},{48,56},{56,48},{64,72... | collective-permute-start | bytes 1966088 | tf_op jit(solution)/shard_map/ppermute | solution.py:19
  82.0 1.9 copy-start.5
  82.0 5.6 %copy-start.20 = (f32[5,4,128,128]{2,3,0,1:T(8,128)S(1)}, f32[5,4,128,128]{2,3,0,1:T(8,128)}, u32[]{:S(2)}) copy-start(f32[5,4,128,128]{2,3,0,1:T(8,128)} %get-tuple-element.40) | copy-start | bytes 3932164
  88.9 61.6 %collective-permute-start.1 = (bf16[4,4,128,128]{2,3,0,1:T(8,128)(2,1)}, bf16[4,4,128,128]{2,3,0,1:T(8,128)(2,1)}, u32[]{:S(2)}, u32[]{:S(2)}) collective-permute-start(bf16[4,4,128,128]{2,3,0,1:T(8,128)(2,1)} %get-tuple-element.28), channel_id=1, source_target_pairs={{0,16},{16,0},{8,24},{24,8},{32,48},{48,32},{40,56},{56,40},{64,80... | collective-permute-start | bytes 1572872 | tf_op jit(solution)/shard_map/ppermute | solution.py:19
  122.8 2.0 copy-start.8
  122.8 2.0 copy-start.18
  123.1 0.8 copy-start.10
  141.7 6.8 %copy-start.4 = (bf16[512,512]{0,1:T(8,128)(2,1)S(1)}, bf16[512,512]{0,1:T(8,128)(2,1)}, u32[]{:S(2)}) copy-start(bf16[512,512]{0,1:T(8,128)(2,1)} %copy-done.3) | copy-start | bytes 1572868
  141.7 55.6 %all-to-all-start.1 = ((bf16[8,512,512]{1,2,0:T(8,128)(2,1)}), bf16[8,512,512]{1,2,0:T(8,128)(2,1)}, u32[]{:S(2)}, u32[]{:S(2)}) async-start(bf16[8,512,512]{1,2,0:T(8,128)(2,1)} %bitcast.98), calls=%async_computation.1 | async-start | bytes 8388608 | tf_op jit(solution)/shard_map/all_to_all | solution.py:29
  148.4 4.2 %copy-start.15 = (f32[4,4,128,128]{2,3,0,1:T(8,128)S(1)}, f32[4,4,128,128]{2,3,0,1:T(8,128)}, u32[]{:S(2)}) copy-start(f32[4,4,128,128]{2,3,0,1:T(8,128)} %get-tuple-element.29) | copy-start | bytes 3145732
  148.4 7.2 %copy-start.9 = (bf16[5,4,128,128]{3,2,1,0:T(8,128)(2,1)S(1)}, bf16[5,4,128,128]{3,2,1,0:T(8,128)(2,1)}, u32[]{:S(2)}) copy-start(bf16[5,4,128,128]{3,2,1,0:T(8,128)(2,1)} %copy-done.8) | copy-start | bytes 1966084
  151.6 1.0 copy-start.14
  153.8 11.5 %collective-permute-start.2 = (bf16[3,4,128,128]{2,3,0,1:T(8,128)(2,1)}, bf16[3,4,128,128]{2,3,0,1:T(8,128)(2,1)}, u32[]{:S(2)}, u32[]{:S(2)}) collective-permute-start(bf16[3,4,128,128]{2,3,0,1:T(8,128)(2,1)} %get-tuple-element.26), channel_id=1, source_target_pairs={{0,32},{32,0},{8,40},{40,8},{16,48},{48,16},{24,56},{56,24},{64,96... | collective-permute-start | bytes 1179656 | tf_op jit(solution)/shard_map/ppermute | solution.py:19
  160.1 6.2 %copy-start.16 = (f32[3,4,128,128]{2,3,0,1:T(8,128)S(1)}, f32[3,4,128,128]{2,3,0,1:T(8,128)}, u32[]{:S(2)}) copy-start(f32[3,4,128,128]{2,3,0,1:T(8,128)} %get-tuple-element.27) | copy-start | bytes 2359300
  160.1 7.9 %copy-start.17 = (f32[5,4,128,128]{2,3,0,1:T(8,128)S(1)}, f32[5,4,128,128]{2,3,0,1:T(8,128)}, u32[]{:S(2)}) copy-start(f32[5,4,128,128]{2,3,0,1:T(8,128)} %fusion.86) | copy-start | bytes 3932164
  166.4 24.8 %copy-start.13 = (f32[512,4,128]{2,0,1:T(8,128)S(1)}, f32[512,4,128]{2,0,1:T(8,128)}, u32[]{:S(2)}) copy-start(f32[512,4,128]{2,0,1:T(8,128)} %convolution_bitcast_fusion) | copy-start | bytes 3145732
  166.4 14.0 %collective-permute-start.3 = (bf16[2,4,128,128]{2,3,0,1:T(8,128)(2,1)S(1)}, bf16[2,4,128,128]{2,3,0,1:T(8,128)(2,1)S(1)}, u32[]{:S(2)}, u32[]{:S(2)}) collective-permute-start(bf16[2,4,128,128]{2,3,0,1:T(8,128)(2,1)S(1)} %get-tuple-element.24), channel_id=1, source_target_pairs={{0,64},{64,0},{8,72},{72,8},{16,80},{80,16},{24,88},{88,24},{32,96... | collective-permute-start | bytes 786440 | tf_op jit(solution)/shard_map/ppermute | solution.py:19
  180.6 10.2 %collective-permute-start.4 = (bf16[1,4,128,128]{2,3,0,1:T(8,128)(2,1)S(1)}, bf16[1,4,128,128]{2,3,0,1:T(8,128)(2,1)S(1)}, u32[]{:S(2)}, u32[]{:S(2)}) collective-permute-start(bf16[1,4,128,128]{2,3,0,1:T(8,128)(2,1)S(1)} %get-tuple-element.32), channel_id=1, source_target_pairs={{0,128},{128,0},{8,136},{136,8},{16,144},{144,16},{24,152},{152,24... | collective-permute-start | bytes 393224 | tf_op jit(solution)/shard_map/ppermute | solution.py:19
  183.4 9.4 %copy-start.7 = (bf16[512,4,128]{2,1,0:T(4,128)(2,1)S(1)}, bf16[512,4,128]{2,1,0:T(4,128)(2,1)}, u32[]{:S(2)}) copy-start(bf16[512,4,128]{2,1,0:T(4,128)(2,1)} %param.7) | copy-start | bytes 1572868
  191.0 2.1 %copy-start.12 = (f32[4,128,512]{2,1,0:T(8,128)S(1)}, f32[4,128,512]{2,1,0:T(8,128)}, u32[]{:S(2)}) copy-start(f32[4,128,512]{2,1,0:T(8,128)} %fusion.120) | copy-start | bytes 3145732
Sparse Core Ops, SparseCore 0:
  9.8 38.7 all-gather.1
